TPU v7x, 128 devices: a whole 4x4x4 slice. The times are simulated.
128 devices in a mesh: row: 8 (over x_lo, y), col: 16 (over x_hi, z, core).
Axes of the slice: x: 4 (x_hi: 2, x_lo: 2; x = x_hi * 2 + x_lo), y: 4, z: 4, core: 2. Of those that a mesh axis runs over, the one named last changes fastest.
Arguments:
- r_vector: bfloat16 [3072, 18432], P(('row', 'col')), may hold values from -100 to 100, as said below
- r_previous: bfloat16 [3072, 18432], P(('row', 'col')), may hold values from -100 to 100, as said below
- cycle_block: bfloat16 [18432, 18432], P('row', 'col'), may hold values from -0.046875 to 0.046875
- ladder_block: bfloat16 [48, 48, 48, 48], P(None, 'col', None, 'row'), may hold values from -0.125 to 0.125
- occ_energy: float32 [48], replicated, may hold values from -3 to -0.5
- vir_energy: float32 [384], replicated, may hold values from 0.3 to 4
- beta_previous: float32 [64], replicated, may hold values from 0.3 to 3
Outputs:
- next_vector: bfloat16 [3072, 18432], P(('row', 'col'))
- alpha_coef: float32 [64], replicated
- beta_coef: float32 [64], replicated
Inputs may be any that keep to these rules, and one draw needn't show every extreme that they name: `r_vector`: real-valued amplitudes, rough from entry to entry. `r_previous`: real-valued amplitudes, rough from entry to entry.
All inputs are finite; a program needn't handle non-finite values.
Results may differ from a plain program's by a relative error of at most 0.001.
Values may be sent and summed in bfloat16 or wider, within the bound.
A program may use at most 128 MiB of HBM per device.

v0:
```python
import jax
import jax.numpy as jnp
from jax import lax
from jax.sharding import PartitionSpec as P

O = 48
V = 384
NVEC = 64


def on_device(
    r_vector, r_previous, cycle_block, ladder_block, occ_energy, vir_energy, beta_previous
):
    n_row = lax.axis_size("row")
    n_col = lax.axis_size("col")
    local_rows = r_vector.shape[0]
    row_width = r_vector.shape[1]
    all_rows = NVEC * O
    j_part = ladder_block.shape[1]
    q_part = ladder_block.shape[3]
    column_part = lax.all_to_all(r_vector, "row", split_axis=1, concat_axis=0, tiled=True)
    shaped = column_part.reshape(n_row, 1, local_rows, column_part.shape[1])
    gathered = lax.all_gather(shaped, "col", axis=1, tiled=True)
    operand = gathered.reshape(all_rows, column_part.shape[1])
    cycle_part = jnp.dot(operand, cycle_block, preferred_element_type=jnp.float32)
    ladder_part = jnp.einsum(
        "ijpq,npqa->nija",
        ladder_block,
        operand.reshape(NVEC, O, q_part, V),
        preferred_element_type=jnp.float32,
    )
    out_width = j_part * V
    partial_value = cycle_part + ladder_part.reshape(all_rows, out_width)
    summed = lax.psum_scatter(
        partial_value.reshape(n_row, n_col, local_rows, out_width),
        "row",
        scatter_dimension=0,
        tiled=True,
    )
    sigma_rows = lax.all_to_all(summed, "col", split_axis=1, concat_axis=3, tiled=True)
    sigma_rows = sigma_rows.reshape(local_rows, row_width)
    linear_index = lax.axis_index("row") * n_col + lax.axis_index("col")
    row_ids = linear_index * local_rows + jnp.arange(local_rows, dtype=jnp.int32)
    occ_index = row_ids % O
    vec_of_row = row_ids // O
    occ_rows = jnp.sum(
        jnp.where(occ_index[:, None] == jnp.arange(O)[None, :], occ_energy[None, :], 0.0), axis=1
    )
    r_float = r_vector.astype(jnp.float32)
    prev_float = r_previous.astype(jnp.float32)
    diagonal = vir_energy[None, None, :] - occ_rows[:, None, None] - occ_energy[None, :, None]
    sigma_rows = sigma_rows + (diagonal * r_float.reshape(local_rows, O, V)).reshape(
        local_rows, row_width
    )
    member = (vec_of_row[:, None] == jnp.arange(NVEC)[None, :]).astype(jnp.float32)
    count_all = O * O * V

    def per_vector(row_sums):
        return jnp.sum(member * row_sums[:, None], axis=0)

    def per_row(coefs):
        return jnp.sum(member * coefs[None, :], axis=1)

    rs_sum, rr_sum = lax.psum(
        (
            per_vector(jnp.sum(r_float * sigma_rows, axis=1)),
            per_vector(jnp.sum(r_float * r_float, axis=1)),
        ),
        ("row", "col"),
    )
    alpha_coef = rs_sum / count_all / (rr_sum / count_all + 1e-06)
    residual_vec = (
        sigma_rows
        - per_row(alpha_coef)[:, None] * r_float
        - per_row(beta_previous)[:, None] * prev_float
    )
    norm_sum = lax.psum(per_vector(jnp.sum(residual_vec * residual_vec, axis=1)), ("row", "col"))
    beta_coef = jnp.sqrt(norm_sum / count_all + 1e-06)
    next_vector = (residual_vec / per_row(beta_coef)[:, None]).astype(jnp.bfloat16)
    return (next_vector, alpha_coef, beta_coef)


def solution(mesh):
    placed = (
        P(("row", "col"), None),
        P(("row", "col"), None),
        P("row", "col"),
        P(None, "col", None, "row"),
        P(),
        P(),
        P(),
    )
    return jax.shard_map(
        on_device,
        mesh=mesh,
        in_specs=placed,
        out_specs=(P(("row", "col"), None), P(), P()),
        check_vma=False,
    )
```

profile of v0, /device:TPU:1, one launch (start us, length us, event | category | flops | bytes accessed | tf_op | source)
XLA Modules:
  0.0 714.6 jit_solution(3815246468868575005)
XLA Ops:
  7.2 0.0 copy-start
  7.2 0.0 all-gather.3.cloned.1.call-start
  7.2 1.3 copy.67
  8.5 18.4 %all_to_all.31 = bf16[24,8,2304]{2,0,1:T(8,128)(2,1)S(1)} all-to-all(bf16[24,8,2304]{2,0,1:T(8,128)(2,1)S(1)} %bitcast.48), channel_id=1, replica_groups=mesh['row'=8,'col'=16] {'row'}, dimensions={1} | all-to-all | bytes 1769472 | tf_op jit(solution)/shard_map/all_to_all | solution.py:21
  26.9 1.1 copy.44
  27.9 0.0 all-gather.3.cloned.1.call-update
  28.0 0.0 all-reduce.4.cloned.1.call-start
  28.0 99.5 %all-gather.3.cloned.1.call-done = bf16[8,384,2304]{2,0,1:T(8,128)(2,1)} async-done(((bf16[8,24,2304]{2,0,1:T(8,128)(2,1)}), bf16[8,384,2304]{2,0,1:T(8,128)(2,1)}) %all-gather.3.cloned.1.call-update) | async-done | bytes 14155792 | tf_op jit(solution)/shard_map/all_gather | solution.py:23
  127.5 15.0 %copy.45 = bf16[8,384,2304]{2,1,0:T(8,128)(2,1)} copy(bf16[8,384,2304]{2,0,1:T(8,128)(2,1)} %all-gather.3.cloned.1.call-done) | data formatting | bytes 28311552 | tf_op jit(solution)/shard_map/all_gather | solution.py:23
  142.6 28.1 %reshape_reshape.3 = bf16[64,48,6,384]{3,2,1,0:T(8,128)(2,1)} reshape(bf16[8,384,2304]{2,1,0:T(8,128)(2,1)} %copy.45) | data formatting | bytes 28311552 | tf_op jit(solution)/shard_map/reshape;reshape | solution.py:29
  170.7 0.0 copy-done
  170.7 13.5 %fusion.2 = f32[64,48,3,384]{3,1,2,0:T(8,128)} fusion(bf16[64,48,6,384,1]{3,2,1,0,4:T(8,128)(2,1)} %bitcast.38, bf16[48,3,48,6]{2,0,3,1:T(8,128)(2,1)S(1)} %copy-done), kind=kOutput, calls=%fused_computation.3 | convolution fusion | flops 2038431744 | bytes 28394496 | tf_op jit(solution)/shard_map/ijpq,npqa->nija/dot_general | solution.py:26
  184.2 16.5 %copy.48 = f32[64,48,3,384]{3,2,1,0:T(4,128)S(1)} copy(f32[64,48,3,384]{3,1,2,0:T(8,128)} %fusion.2) | data formatting | bytes 28311552 | tf_op jit(solution)/shard_map/ijpq,npqa->nija/transpose | solution.py:26
  200.7 0.0 slice-start.2
  200.7 0.0 slice-start.3
  200.7 6.7 copy.58
  207.4 0.0 slice-done
  207.4 0.0 slice-done.1
  207.4 0.0 slice-done.2
  207.4 0.0 slice-done.3
  207.4 24.9 %convolution_add_fusion = f32[3072,1152]{1,0:T(8,128)} fusion(f32[3072,1152]{1,0:T(8,128)} %bitcast.44, bf16[3072,2304]{1,0:T(8,128)(2,1)S(1)} %bitcast.37, bf16[2304,1152]{1,0:T(8,128)(2,1)} %param.9), kind=kOutput, calls=%fused_computation.2 | convolution fusion | flops 16310992896 | bytes 47775744 | tf_op jit(solution)/shard_map/dot_general | solution.py:25
  232.3 11.5 %copy.49 = f32[8,16,24,1152]{3,2,0,1:T(8,128)} copy(f32[8,16,24,1152]{3,2,1,0:T(8,128)} %bitcast.43) | data formatting | bytes 28311552 | tf_op jit(solution)/shard_map/reshape | solution.py:35
  243.8 0.0 all-reduce.4.cloned.1.call-update
  243.8 0.6 copy-done.8
  244.4 0.6 dynamic-slice
  245.0 288.9 %all-reduce.4.cloned.1.call-done = f32[8,16,24,1152]{3,2,0,1:T(8,128)} async-done(((f32[8,16,24,1152]{3,2,0,1:T(8,128)}), f32[8,16,24,1152]{3,2,0,1:T(8,128)}) %all-reduce.4.cloned.1.call-update) | async-done | bytes 14155792
  533.9 3.4 constant_dynamic-slice_fusion
  537.4 7.5 %all-to-all-start.1 = ((f32[1,16,24,1152]{3,2,0,1:T(8,128)}), f32[1,16,24,1152]{3,2,0,1:T(8,128)}, u32[]{:S(2)}, u32[]{:S(2)}) async-start(f32[1,16,24,1152]{3,2,0,1:T(8,128)} %constant_dynamic-slice_fusion), calls=%async_computation.1 | async-start | bytes 3538944 | tf_op jit(solution)/shard_map/all_to_all | solution.py:40
  544.9 0.0 copy-done.5
  544.9 0.2 select_reduce_fusion.6
  545.1 0.1 broadcast_subtract_fusion
  545.2 0.1 sub.51
  545.3 0.6 copy.60
  545.9 0.1 sub.53
  546.0 23.9 %all-to-all-done.1 = f32[1,16,24,1152]{3,2,0,1:T(8,128)} async-done(((f32[1,16,24,1152]{3,2,0,1:T(8,128)}), f32[1,16,24,1152]{3,2,0,1:T(8,128)}, u32[]{:S(2)}, u32[]{:S(2)}) %all-to-all-start.1) | async-done | bytes 1769504 | tf_op jit(solution)/shard_map/all_to_all | solution.py:40
  569.8 1.7 copy.59
  571.5 0.0 copy-start.2
  571.5 1.2 copy-done.2
  572.7 0.8 fusion.6
  573.6 0.1 select_reduce_fusion.5
  573.7 64.7 %all-reduce.1 = (f32[64]{0:T(128)S(1)}, f32[64]{0:T(128)S(1)}) all-reduce(f32[64]{0:T(128)S(1)} %get-tuple-element.8, f32[64]{0:T(128)S(1)} %get-tuple-element.7), channel_id=1, replica_groups=mesh['row'=8,'col'=16] {'row','col'}, use_global_device_ids=true, to_apply=%region_7.8 | all-reduce | flops 128 | bytes 1024 | tf_op jit(solution)/shard_map/psum | solution.py:64
  638.4 0.2 select_reduce_fusion.3
  638.5 3.8 multiply_reduce_fusion
  642.4 0.0 copy-done.7
  642.4 0.1 select_reduce_fusion.1
  642.5 62.5 %psum.23 = f32[64]{0:T(128)S(1)} all-reduce(f32[64]{0:T(128)S(1)} %select_reduce_fusion.1), channel_id=1, replica_groups=mesh['row'=8,'col'=16] {'row','col'}, use_global_device_ids=true, to_apply=%region_12.13 | all-reduce | flops 64 | bytes 512 | tf_op jit(solution)/shard_map/psum | solution.py:77
  705.0 0.2 select_reduce_fusion
  705.2 2.6 divide_convert_fusion
  (20 shorter events, 0.1 us)
Async XLA Ops:
  7.2 163.5 %copy-start = (bf16[48,3,48,6]{2,0,3,1:T(8,128)(2,1)S(1)}, bf16[48,3,48,6]{2,0,3,1:T(8,128)(2,1)}, u32[]{:S(2)}) copy-start(bf16[48,3,48,6]{2,0,3,1:T(8,128)(2,1)} %param.10) | copy-start | bytes 248836
  7.2 120.4 %all-gather.3.cloned.1.call-start = ((), (), s32[]{:S(2)}) async-start(), calls=%async_computation.2 | async-start | bytes 15040512 | tf_op jit(solution)/shard_map/all_gather | solution.py:23
  28.0 506.0 %all-reduce.4.cloned.1.call-start = ((), (), s32[]{:S(2)}) async-start(), calls=%async_computation.3 | async-start | bytes 28311552
  184.2 23.2 %slice-start = ((s8[14155776]{0:T(1024)(128)(4,1)}), s8[4194304]{0:T(1024)(128)(4,1)S(1)}, s32[]{:S(2)}) async-start(s8[14155776]{0:T(1024)(128)(4,1)} %bitcast.35), calls=%async_computation.4 | async-start | bytes 8388608
  184.2 23.2 %slice-start.1 = ((s8[14155776]{0:T(1024)(128)(4,1)}), s8[4194304]{0:T(1024)(128)(4,1)S(1)}, s32[]{:S(2)}) async-start(s8[14155776]{0:T(1024)(128)(4,1)} %bitcast.35), calls=%async_computation.5 | async-start | bytes 8388608
  200.7 6.7 slice-start.2
  200.7 6.7 slice-start.3
  243.8 0.7 copy-start.8
  537.4 7.6 %copy-start.5 = (f32[48]{0:T(128)S(1)}, f32[48]{0:T(128)}, u32[]{:S(2)}) copy-start(f32[48]{0:T(128)} %param.11) | copy-start | bytes 580
  537.4 7.7 %copy-start.4 = (f32[384]{0:T(512)S(1)}, f32[384]{0:T(512)}, u32[]{:S(2)}) copy-start(f32[384]{0:T(512)} %param.12) | copy-start | bytes 4612
  537.4 32.5 %all-to-all-start.1 = ((f32[1,16,24,1152]{3,2,0,1:T(8,128)}), f32[1,16,24,1152]{3,2,0,1:T(8,128)}, u32[]{:S(2)}, u32[]{:S(2)}) async-start(f32[1,16,24,1152]{3,2,0,1:T(8,128)} %constant_dynamic-slice_fusion), calls=%async_computation.1 | async-start | bytes 3538944 | tf_op jit(solution)/shard_map/all_to_all | solution.py:40
  569.8 2.9 copy-start.3
  571.5 1.2 copy-start.2
  572.7 65.6 %copy-start.6 = (f32[64]{0:T(128)S(1)}, f32[64]{0:T(128)}, u32[]{:S(2)}) copy-start(f32[64]{0:T(128)} %param.13) | copy-start | bytes 772
  638.3 4.0 copy-start.7
  638.5 69.2 %copy-start.1 = (bf16[48,3,48,6]{2,0,3,1:T(8,128)(2,1)S(1)}, bf16[48,3,48,6]{2,0,3,1:T(8,128)(2,1)}, u32[]{:S(2)}) copy-start(bf16[48,3,48,6]{2,0,3,1:T(8,128)(2,1)} %param.10) | copy-start | bytes 248836
  705.0 2.8 copy-start.9
Sparse Core Ops, SparseCore 0:
  28.1 99.4 all-gather.2
  243.9 289.9 all-reduce.3
where the time goes:
time: 716 us; the launch traced here: 715 us
  waiting for transfers between devices  412 us (58%)
  blocking collectives  146 us (20%)
  local copies, waits for them, and re-layouts  88.4 us (12%)
  matrix products  38.4 us (5%)
  between operations  14.2 us (2%)
  other arithmetic  8.04 us (1%)
  starting transfers between devices  7.61 us (1%)
    unnamed x3, waiting for transfers between devices  289 us
    all_gather x1, waiting for transfers between devices, on_device(): gathered = lax.all_gather(shaped, 'col', axis=1, tiled=True)  99.5 us
    psum x1, blocking collectives, on_device(): lax.psum((per_vector(jnp.sum(r_float * sigma_rows, axis=1)), per_vector(j...  64.7 us
    psum x1, blocking collectives, on_device(): lax.psum(per_vector(jnp.sum(residual_vec * residual_vec, axis=1)), ('row'...  62.5 us
    another operation x1, local copies, waits for them, and re-layouts, on_device(): operand.reshape(NVEC, O, q_part, V)  28.1 us
    dot_general x1, matrix products, on_device(): jnp.dot(operand, cycle_block, preferred_element_type=jnp.float32)  24.9 us
    all_to_all x1, waiting for transfers between devices, on_device(): lax.all_to_all(summed, 'col', split_axis=1, concat_axis=3, tiled=True)  23.9 us
    all_to_all x1, blocking collectives, on_device(): lax.all_to_all(r_vector, 'row', split_axis=1, concat_axis=0, tiled=True)  18.4 us
  transfers between devices with their start and end apart: 3, of which 3 were waited for; matrix products, arithmetic and copies ran while one was open for 0% of the time, Pallas kernels for 0%

commit v1 on v0

--- a/solution.py
+++ b/solution.py
@@ -6,6 +6,19 @@
 O = 48
 V = 384
 NVEC = 64
+
+
+def mix_ports_on(my_tile, mesh_name):
+    big = jnp.concatenate(
+        jax.lax.all_to_all(
+            jnp.stack([my_tile for _ in range(jax.lax.axis_size(mesh_name))], 0),
+            axis_name=mesh_name,
+            split_axis=0,
+            concat_axis=0,
+        ),
+        1,
+    )
+    return big
 
 
 def on_device(
@@ -20,7 +33,7 @@
     q_part = ladder_block.shape[3]
     column_part = lax.all_to_all(r_vector, "row", split_axis=1, concat_axis=0, tiled=True)
     shaped = column_part.reshape(n_row, 1, local_rows, column_part.shape[1])
-    gathered = lax.all_gather(shaped, "col", axis=1, tiled=True)
+    gathered = mix_ports_on(shaped, mesh_name="col")
     operand = gathered.reshape(all_rows, column_part.shape[1])
     cycle_part = jnp.dot(operand, cycle_block, preferred_element_type=jnp.float32)
     ladder_part = jnp.einsum(

time: 716 us -> 779 us (1.088)
  blocking collectives: 146 us -> 313 us
  waiting for transfers between devices: 412 us -> 313 us
    all_to_all x0 -> x1, blocking collectives: none -> 167 us  [mix_ports_on(): jax.lax.all_to_all(jnp.stack([my_tile for _ in range(jax.lax.axis_size(me...]
    all_gather x1 -> x0, waiting for transfers between devices: 99.5 us -> none  [on_device(): gathered = lax.all_gather(shaped, 'col', axis=1, tiled=True)]
    all_gather x1 -> x0, local copies, waits for them, and re-layouts: 15 us -> none  [on_device(): gathered = lax.all_gather(shaped, 'col', axis=1, tiled=True)]
    unnamed x3 -> x2, waiting for transfers between devices: 289 us -> 289 us
  transfers between devices with their start and end apart: 3 -> 2, of which waited for: 3 -> 2; matrix products, arithmetic and copies ran while one was open for 0% -> 0% of each run, Pallas kernels for 0% -> 0%
where the time goes in v1:
time: 779 us; the launch traced here: 778 us
  blocking collectives  313 us (40%)
  waiting for transfers between devices  313 us (40%)
  local copies, waits for them, and re-layouts  84.4 us (11%)
  matrix products  38.4 us (5%)
  between operations  14.2 us (2%)
  other arithmetic  8.04 us (1%)
    unnamed x2, waiting for transfers between devices  289 us
    all_to_all x1, blocking collectives, mix_ports_on(): jax.lax.all_to_all(jnp.stack([my_tile for _ in range(jax.lax.axis_size(me...  167 us
    psum x1, blocking collectives, on_device(): lax.psum((per_vector(jnp.sum(r_float * sigma_rows, axis=1)), per_vector(j...  64.7 us
    psum x1, blocking collectives, on_device(): lax.psum(per_vector(jnp.sum(residual_vec * residual_vec, axis=1)), ('row'...  62.5 us
    another operation x1, local copies, waits for them, and re-layouts, on_device(): operand.reshape(NVEC, O, q_part, V)  28.1 us
    dot_general x1, matrix products, on_device(): jnp.dot(operand, cycle_block, preferred_element_type=jnp.float32)  24.9 us
    all_to_all x1, waiting for transfers between devices, on_device(): lax.all_to_all(summed, 'col', split_axis=1, concat_axis=3, tiled=True)  23.9 us
    all_to_all x1, blocking collectives, on_device(): lax.all_to_all(r_vector, 'row', split_axis=1, concat_axis=0, tiled=True)  18.4 us
  transfers between devices with their start and end apart: 2, of which 2 were waited for; matrix products, arithmetic and copies ran while one was open for 0% of the time, Pallas kernels for 0%

profile of v1, /device:TPU:1, one launch (start us, length us, event | category | flops | bytes accessed | tf_op | source)
XLA Modules:
  0.0 777.9 jit_solution(10879410886352704305)
XLA Ops:
  7.2 0.0 copy-start
  7.2 0.0 all-reduce.4.cloned.1.call-start
  7.2 1.3 copy.58
  8.5 18.4 %all_to_all.36 = bf16[24,8,2304]{2,0,1:T(8,128)(2,1)S(1)} all-to-all(bf16[24,8,2304]{2,0,1:T(8,128)(2,1)S(1)} %bitcast.55), channel_id=1, replica_groups=mesh['row'=8,'col'=16] {'row'}, dimensions={1} | all-to-all | bytes 1769472 | tf_op jit(solution)/shard_map/all_to_all | solution.py:34
  26.9 6.5 stack.3
  33.4 167.1 %all_to_all.37 = bf16[16,8,1,24,2304]{4,3,1,2,0:T(8,128)(2,1)S(1)} all-to-all(bf16[16,8,1,24,2304]{4,3,1,2,0:T(8,128)(2,1)} %stack.3), channel_id=1, replica_groups=mesh['row'=8,'col'=16] {'col'}, dimensions={0} | all-to-all | bytes 28311552 | tf_op jit(solution)/shard_map/all_to_all | solution.py:13
  200.4 5.5 copy.59
  206.0 28.1 %reshape_reshape_reshape.3 = bf16[64,48,6,384]{3,2,1,0:T(8,128)(2,1)} reshape(bf16[8,16,1,24,2304]{4,3,1,0,2:T(8,128)(2,1)} %bitcast.42) | data formatting | bytes 28311552 | tf_op jit(solution)/shard_map/reshape;reshape;reshape | solution.py:42
  234.1 0.0 copy-done
  234.1 13.5 %fusion.2 = f32[64,48,3,384]{3,1,2,0:T(8,128)} fusion(bf16[64,48,6,384,1]{3,2,1,0,4:T(8,128)(2,1)} %bitcast.46, bf16[48,3,48,6]{2,0,3,1:T(8,128)(2,1)S(1)} %copy-done), kind=kOutput, calls=%fused_computation.3 | convolution fusion | flops 2038431744 | bytes 28394496 | tf_op jit(solution)/shard_map/ijpq,npqa->nija/dot_general | solution.py:39
  247.6 16.5 %copy.37 = f32[64,48,3,384]{3,2,1,0:T(4,128)S(1)} copy(f32[64,48,3,384]{3,1,2,0:T(8,128)} %fusion.2) | data formatting | bytes 28311552 | tf_op jit(solution)/shard_map/ijpq,npqa->nija/transpose | solution.py:39
  264.1 0.0 slice-start.2
  264.1 0.0 slice-start.3
  264.1 6.7 copy.47
  270.8 0.0 slice-done
  270.8 0.0 slice-done.1
  270.8 0.0 slice-done.2
  270.8 0.0 slice-done.3
  270.9 24.9 %convolution_add_fusion = f32[3072,1152]{1,0:T(8,128)} fusion(f32[3072,1152]{1,0:T(8,128)} %bitcast.52, bf16[3072,2304]{1,0:T(8,128)(2,1)S(1)} %bitcast.45, bf16[2304,1152]{1,0:T(8,128)(2,1)} %param.9), kind=kOutput, calls=%fused_computation.2 | convolution fusion | flops 16310992896 | bytes 47775744 | tf_op jit(solution)/shard_map/dot_general | solution.py:38
  295.7 11.5 %copy.38 = f32[8,16,24,1152]{3,2,0,1:T(8,128)} copy(f32[8,16,24,1152]{3,2,1,0:T(8,128)} %bitcast.51) | data formatting | bytes 28311552 | tf_op jit(solution)/shard_map/reshape | solution.py:48
  307.2 0.0 all-reduce.4.cloned.1.call-update
  307.2 0.6 copy-done.8
  307.8 0.6 dynamic-slice
  308.4 288.7 %all-reduce.4.cloned.1.call-done = f32[8,16,24,1152]{3,2,0,1:T(8,128)} async-done(((f32[8,16,24,1152]{3,2,0,1:T(8,128)}), f32[8,16,24,1152]{3,2,0,1:T(8,128)}) %all-reduce.4.cloned.1.call-update) | async-done | bytes 14155792
  597.1 3.4 constant_dynamic-slice_fusion
  600.5 7.7 all-to-all-start.2
  608.2 0.0 copy-done.5
  608.2 0.2 select_reduce_fusion.6
  608.4 0.0 copy-done.4
  608.4 0.1 broadcast_subtract_fusion
  608.5 0.1 sub.51
  608.6 0.6 copy.49
  609.2 0.1 sub.53
  609.3 23.9 %all-to-all-done.2 = f32[1,16,24,1152]{3,2,0,1:T(8,128)} async-done(((f32[1,16,24,1152]{3,2,0,1:T(8,128)}), f32[1,16,24,1152]{3,2,0,1:T(8,128)}, u32[]{:S(2)}, u32[]{:S(2)}) %all-to-all-start.2) | async-done | bytes 1769504 | tf_op jit(solution)/shard_map/all_to_all | solution.py:53
  633.1 1.7 copy.48
  634.8 0.0 copy-start.2
  634.8 1.2 copy-done.2
  636.0 0.0 copy-done.3
  636.0 0.8 fusion.6
  636.9 0.1 select_reduce_fusion.5
  637.0 64.7 %all-reduce.1 = (f32[64]{0:T(128)S(1)}, f32[64]{0:T(128)S(1)}) all-reduce(f32[64]{0:T(128)S(1)} %get-tuple-element.8, f32[64]{0:T(128)S(1)} %get-tuple-element.7), channel_id=1, replica_groups=mesh['row'=8,'col'=16] {'row','col'}, use_global_device_ids=true, to_apply=%region_7.8 | all-reduce | flops 128 | bytes 1024 | tf_op jit(solution)/shard_map/psum | solution.py:77
  701.6 0.0 copy-done.6
  701.7 0.2 select_reduce_fusion.3
  701.8 3.8 multiply_reduce_fusion
  705.7 0.1 select_reduce_fusion.1
  705.8 62.5 %psum.23 = f32[64]{0:T(128)S(1)} all-reduce(f32[64]{0:T(128)S(1)} %select_reduce_fusion.1), channel_id=1, replica_groups=mesh['row'=8,'col'=16] {'row','col'}, use_global_device_ids=true, to_apply=%region_12.13 | all-reduce | flops 64 | bytes 512 | tf_op jit(solution)/shard_map/psum | solution.py:90
  768.3 0.2 select_reduce_fusion
  768.5 2.6 divide_convert_fusion
  (18 shorter events, 0.1 us)
Async XLA Ops:
  7.2 226.9 %copy-start = (bf16[48,3,48,6]{2,0,3,1:T(8,128)(2,1)S(1)}, bf16[48,3,48,6]{2,0,3,1:T(8,128)(2,1)}, u32[]{:S(2)}) copy-start(bf16[48,3,48,6]{2,0,3,1:T(8,128)(2,1)} %param.10) | copy-start | bytes 248836
  7.2 589.9 %all-reduce.4.cloned.1.call-start = ((), (), s32[]{:S(2)}) async-start(), calls=%async_computation.3 | async-start | bytes 28311552
  247.6 23.2 %slice-start = ((s8[14155776]{0:T(1024)(128)(4,1)}), s8[4194304]{0:T(1024)(128)(4,1)S(1)}, s32[]{:S(2)}) async-start(s8[14155776]{0:T(1024)(128)(4,1)} %bitcast.43), calls=%async_computation.4 | async-start | bytes 8388608
  247.6 23.2 %slice-start.1 = ((s8[14155776]{0:T(1024)(128)(4,1)}), s8[4194304]{0:T(1024)(128)(4,1)S(1)}, s32[]{:S(2)}) async-start(s8[14155776]{0:T(1024)(128)(4,1)} %bitcast.43), calls=%async_computation.5 | async-start | bytes 8388608
  264.1 6.7 slice-start.2
  264.1 6.7 slice-start.3
  307.2 0.7 copy-start.8
  600.5 7.7 copy-start.5
  600.5 7.9 %copy-start.4 = (f32[384]{0:T(512)S(1)}, f32[384]{0:T(512)}, u32[]{:S(2)}) copy-start(f32[384]{0:T(512)} %param.12) | copy-start | bytes 4612
  600.5 32.6 %all-to-all-start.2 = ((f32[1,16,24,1152]{3,2,0,1:T(8,128)}), f32[1,16,24,1152]{3,2,0,1:T(8,128)}, u32[]{:S(2)}, u32[]{:S(2)}) async-start(f32[1,16,24,1152]{3,2,0,1:T(8,128)} %constant_dynamic-slice_fusion), calls=%async_computation.2 | async-start | bytes 3538944 | tf_op jit(solution)/shard_map/all_to_all | solution.py:53
  633.1 2.9 copy-start.3
  634.8 1.2 copy-start.2
  636.0 65.6 %copy-start.6 = (f32[64]{0:T(128)S(1)}, f32[64]{0:T(128)}, u32[]{:S(2)}) copy-start(f32[64]{0:T(128)} %param.13) | copy-start | bytes 772
  701.6 4.0 copy-start.7
  701.8 69.2 %copy-start.1 = (bf16[48,3,48,6]{2,0,3,1:T(8,128)(2,1)S(1)}, bf16[48,3,48,6]{2,0,3,1:T(8,128)(2,1)}, u32[]{:S(2)}) copy-start(bf16[48,3,48,6]{2,0,3,1:T(8,128)(2,1)} %param.10) | copy-start | bytes 248836
  768.3 2.8 copy-start.9
Sparse Core Ops, SparseCore 0:
  307.3 289.6 all-reduce.3
